TPU v7x, 32 devices: a whole 2x2x4 slice. The times are simulated.
32 devices in a mesh: img: 8 (over y, x, core), own: 4 (over z).
Axes of the slice: x: 2, y: 2, z: 4, core: 2. Of those that a mesh axis runs over, the one named last changes fastest.
Arguments:
- patches: bfloat16 [6272, 4608], P(('img', 'own')), may hold values from -6 to 6
- grads: bfloat16 [6272, 512], P(('img', 'own')), may hold values from -0.8984375 to 0.8984375
- basis_g: bfloat16 [512, 512], replicated, may hold values from -0.25 to 0.25
- basis_slots: bfloat16 [4608, 9216], P(None, 'own'), may hold values from -0.09375 to 0.09375
- col_counts: int32 [4], replicated, may hold values from 1 to 2304, 4608 in all
Outputs:
- corrections: float32 [4608, 512], P(('img', 'own'))
Inputs may be any that keep to these rules, and one draw needn't show every extreme that they name: `col_counts`: the counts sum to 4608; one owner has exactly 2304.
All inputs are finite; a program needn't handle non-finite values.
Results may differ from a plain program's by a relative error of at most 0.00049.
Values may be sent and summed in bfloat16 or wider, within the bound.
A program may use at most 128 MiB of HBM per device.

v0:
```python
import jax
import jax.numpy as jnp
from jax import lax
from jax.sharding import PartitionSpec as P

POS = 49


def shards(patches, grads, basis_g, basis_slots, col_counts):
    groups = lax.axis_size("img")
    owner_id = lax.axis_index("own")
    slots = basis_slots.shape[1]
    kin = basis_slots.shape[0]
    gout = basis_g.shape[1]
    proj_local = jnp.dot(grads, basis_g, preferred_element_type=jnp.float32).astype(jnp.bfloat16)
    proj_g = lax.all_gather(proj_local, "own", axis=0, tiled=True)
    proj_a = jnp.dot(
        lax.all_gather(patches, "own", axis=0, tiled=True),
        basis_slots,
        preferred_element_type=jnp.float32,
    ).astype(jnp.bfloat16)
    images_here = proj_a.shape[0] // POS
    coef = jnp.einsum(
        "nps,npg->nsg",
        proj_a.reshape(images_here, POS, slots),
        proj_g.reshape(images_here, POS, gout),
        preferred_element_type=jnp.float32,
    )
    total_images = images_here * groups
    slot_corr = jnp.sum(coef * coef, axis=0) / jnp.float32(total_images)
    starts = jnp.cumsum(col_counts) - col_counts
    my_count = lax.dynamic_index_in_dim(col_counts, owner_id, keepdims=False)
    my_start = lax.dynamic_index_in_dim(starts, owner_id, keepdims=False)
    slot_index = jnp.arange(slots, dtype=jnp.int32)
    summed = lax.psum(slot_corr, "img")
    masked = jnp.where((slot_index < my_count)[:, None], summed, jnp.float32(0.0))
    laid = lax.dynamic_update_slice(
        jnp.zeros((kin + slots, gout), jnp.float32), masked, (my_start, jnp.int32(0))
    )[:kin]
    group_rows = kin // groups
    group_start = lax.axis_index("img") * group_rows
    kept = lax.dynamic_slice_in_dim(laid, group_start, group_rows, 0)
    return lax.psum_scatter(kept, "own", scatter_dimension=0, tiled=True)


def solution(mesh):
    in_specs = (P(("img", "own"), None), P(("img", "own"), None), P(), P(None, "own"), P())
    out_specs = P(("img", "own"), None)
    return jax.shard_map(shards, mesh=mesh, in_specs=in_specs, out_specs=out_specs, check_vma=False)
```

profile of v0, /device:TPU:1, one launch (start us, length us, event | category | flops | bytes accessed | tf_op | source)
XLA Modules:
  0.0 349.3 jit_solution(7780667844331035668)
XLA Ops:
  6.5 0.0 copy-start
  6.5 0.0 all-gather.4.cloned.1.call-start
  6.5 0.7 all-gather.4.cloned.1.call-update
  7.3 0.0 all-reduce.2.cloned.1.call-start
  7.3 0.3 copy-done
  7.6 1.2 fusion
  8.8 22.4 %all-gather.1 = bf16[4,196,512]{2,1,0:T(8,128)(2,1)S(1)} all-gather(bf16[1,196,512]{2,1,0:T(8,128)(2,1)S(1)} %fusion), channel_id=1, replica_groups=mesh['img'=8,'own'=4] {'own'}, dimensions={0}, use_global_device_ids=true | all-gather | bytes 1003520 | tf_op jit(solution)/shard_map/all_gather | solution.py:16
  31.2 0.2 reshape.37
  31.4 116.2 %all-gather.4.cloned.1.call-done = bf16[4,196,4608]{2,1,0:T(8,128)(2,1)} async-done(((bf16[1,196,4608]{2,1,0:T(8,128)(2,1)}), bf16[4,196,4608]{2,1,0:T(8,128)(2,1)}) %all-gather.4.cloned.1.call-update) | async-done | bytes 7225360 | tf_op jit(solution)/shard_map/all_gather | solution.py:18
  147.6 5.8 %reshape.41 = bf16[784,4608]{1,0:T(8,128)(2,1)} reshape(bf16[4,196,4608]{2,1,0:T(8,128)(2,1)} %all-gather.4.cloned.1.call-done) | data formatting | bytes 14450688
  153.4 23.4 %convolution_convert_fusion = bf16[784,2304]{1,0:T(8,128)(2,1)} fusion(bf16[784,4608]{1,0:T(8,128)(2,1)} %reshape.41, bf16[4608,2304]{1,0:T(8,128)(2,1)} %param.8), kind=kOutput, calls=%fused_computation.1 | convolution fusion | flops 16648998912 | bytes 32071680 | tf_op jit(solution)/shard_map/dot_general | solution.py:17
  176.8 4.0 %reshape.36 = bf16[16,49,2304]{2,1,0:T(8,128)(2,1)} reshape(bf16[784,2304]{1,0:T(8,128)(2,1)} %convolution_convert_fusion) | data formatting | bytes 7225344 | tf_op jit(solution)/shard_map/reshape | solution.py:25
  180.8 13.2 %multiply_reduce_fusion = f32[2304,512]{1,0:T(8,128)S(1)} fusion(bf16[16,49,2304]{2,1,0:T(8,128)(2,1)} %reshape.36, bf16[16,49,512]{2,1,0:T(8,128)(2,1)S(1)} %reshape.37), kind=kOutput, calls=%fused_computation | convolution fusion | flops 1886257152 | bytes 9134080 | tf_op jit(solution)/shard_map/nps,npg->nsg/dot_general | solution.py:23
  194.0 2.7 broadcast_multiply_fusion
  196.7 0.0 copy-start.2
  196.7 0.0 all-reduce.2.cloned.1.call-update
  196.7 0.2 reduce-scatter.2.cloned.1.call-start
  197.0 0.4 copy-done.2
  197.4 0.6 dynamic_slice.10
  197.9 0.2 reduce-window.9
  198.1 0.7 dynamic_slice.11
  200.8 0.7 iota_compare_fusion
  201.5 81.4 %all-reduce.2.cloned.1.call-done = f32[2304,512]{1,0:T(8,128)} async-done(((f32[2304,512]{1,0:T(8,128)}), f32[2304,512]{1,0:T(8,128)}) %all-reduce.2.cloned.1.call-update) | async-done | bytes 4718608 | tf_op jit(solution)/shard_map/psum | solution.py:35
  282.9 4.4 %broadcast_select_fusion = f32[2304,512]{1,0:T(8,128)} fusion(f32[2304,512]{1,0:T(8,128)} %all-reduce.2.cloned.1.call-done, pred[2304]{0:T(1024)(128)(4,1)S(1)} %iota_compare_fusion), kind=kLoop, calls=%fused_computation.2 | loop fusion | flops 1179648 | bytes 9439488 | tf_op jit(solution)/shard_map/jit(_where)/select_n | solution.py:36
  287.3 6.9 %broadcast_in_dim.16 = f32[6912,512]{1,0:T(8,128)} broadcast(f32[]{:T(128)} %constant.10.clone.1), dimensions={} | broadcast | bytes 14155780 | tf_op jit(solution)/shard_map/broadcast_in_dim | solution.py:38
  294.2 13.2 %dynamic_update_slice.3 = f32[6912,512]{1,0:T(8,128)} dynamic-update-slice(f32[6912,512]{1,0:T(8,128)} %broadcast_in_dim.16, f32[2304,512]{1,0:T(8,128)} %broadcast_select_fusion, s32[]{:T(128)S(6)} %select_n.17, s32[]{:T(128)} %constant.13.clone.1) | dynamic-update-slice | bytes 9437188 | tf_op jit(solution)/shard_map/dynamic_update_slice | solution.py:37
  307.4 0.0 copy-start.1
  307.4 4.9 %slice.4 = f32[4608,512]{1,0:T(8,128)S(1)} slice(f32[6912,512]{1,0:T(8,128)} %dynamic_update_slice.3), slice={[0:4608], [0:512]} | slice | bytes 18874368 | tf_op jit(solution)/shard_map/slice | solution.py:37
  312.2 1.1 constant_dynamic-slice_fusion
  313.3 0.0 reduce-scatter.2.cloned.1.call-update
  313.4 29.4 %reduce-scatter.2.cloned.1.call-done = f32[144,512]{1,0:T(8,128)} async-done(((f32[576,512]{1,0:T(8,128)}), f32[144,512]{1,0:T(8,128)}) %reduce-scatter.2.cloned.1.call-update) | async-done | bytes 294928 | tf_op jit(solution)/shard_map/reduce_scatter | solution.py:43
  342.8 0.0 copy-done.1
  (1 shorter events, 0.0 us)
Async XLA Ops:
  6.5 1.0 copy-start
  6.5 141.1 %all-gather.4.cloned.1.call-start = ((), (), s32[]{:S(2)}) async-start(), calls=%async_computation.3 | async-start | bytes 9216000 | tf_op jit(solution)/shard_map/all_gather | solution.py:18
  7.3 275.6 %all-reduce.2.cloned.1.call-start = ((), (), s32[]{:S(2)}) async-start(), calls=%async_computation.1 | async-start | bytes 9437184 | tf_op jit(solution)/shard_map/psum | solution.py:35
  196.7 0.7 copy-start.2
  196.7 146.1 %reduce-scatter.2.cloned.1.call-start = ((), (), s32[]{:S(2)}) async-start(), calls=%async_computation.2 | async-start | bytes 1474560 | tf_op jit(solution)/shard_map/reduce_scatter | solution.py:43
  307.4 35.4 %copy-start.1 = (bf16[512,512]{1,0:T(8,128)(2,1)S(1)}, bf16[512,512]{1,0:T(8,128)(2,1)}, u32[]{:S(2)}) copy-start(bf16[512,512]{1,0:T(8,128)(2,1)} %param.7) | copy-start | bytes 1572868
Sparse Core Ops, SparseCore 0:
  8.9 138.6 all-gather.3
  196.8 85.9 all-reduce.1
  313.5 29.2 reduce-scatter.1
where the time goes:
time: 351 us; the launch traced here: 349 us
  waiting for transfers between devices  228 us (65%)
  local copies, waits for them, and re-layouts  37.9 us (11%)
  matrix products  37.8 us (11%)
  blocking collectives  22.4 us (6%)
  between operations  15.2 us (4%)
  other arithmetic  7.97 us (2%)
    all_gather x1, waiting for transfers between devices, shards(): lax.all_gather(patches, 'own', axis=0, tiled=True)  116 us
    psum x1, waiting for transfers between devices, shards(): summed = lax.psum(slot_corr, 'img')  81.4 us
    reduce_scatter x1, waiting for transfers between devices, shards(): return lax.psum_scatter(kept, 'own', scatter_dimension=0, tiled=True)  29.4 us
    dot_general x1, matrix products, shards(): jnp.dot(lax.all_gather(patches, 'own', axis=0, tiled=True), basis_slots,...  23.4 us
    all_gather x1, blocking collectives, shards(): proj_g = lax.all_gather(proj_local, 'own', axis=0, tiled=True)  22.4 us
    dynamic_update_slice x1, local copies, waits for them, and re-layouts, shards(): lax.dynamic_update_slice(jnp.zeros((kin + slots, gout), jnp.float32), mas...  13.2 us
    dot_general x1, matrix products, shards(): jnp.einsum('nps,npg->nsg', proj_a.reshape(images_here, POS, slots), proj_...  13.2 us
  transfers between devices with their start and end apart: 3, of which 3 were waited for; matrix products, arithmetic and copies ran while one was open for 1% of the time, Pallas kernels for 0%

commit v1 on v0

v1 whole, which is shorter than its diff:
```python
import functools

import jax
import jax.numpy as jnp
from jax import lax
from jax.experimental import pallas as pl
from jax.experimental.pallas import tpu as pltpu
from jax.sharding import PartitionSpec as P

POS = 49
PIECE = 768
MESH = pl.DeviceIdType.MESH


def widest(total, most):
    return max(w for w in range(128, most + 1, 128) if total % w == 0)


def project(n, images, x_hbm, g_hbm, bg_ref, b_hbm, corr, xbuf, gbuf, bbuf, acc, proj, masked,
            x_sem, g_sem, b_sem, recv, g_recv, right_sem, left_sem, g_right, g_left):
    me = lax.axis_index("own")
    pieces, width, slots = bbuf.shape
    rows = x_hbm.shape[0]
    gout = bg_ref.shape[1]
    tile = widest(slots, 768)
    strip = widest(slots, 256)
    has_left, has_right = me > 0, me < n - 1

    def own_piece(q):
        return pltpu.make_async_copy(
            x_hbm.at[:, pl.ds(pl.multiple_of(q * width, width), width)], xbuf.at[me, q], x_sem.at[q])

    def basis_piece(q):
        return pltpu.make_async_copy(
            b_hbm.at[pl.ds(pl.multiple_of(q * width, width), width)], bbuf.at[q], b_sem.at[q])

    own_g = pltpu.make_async_copy(g_hbm, gbuf.at[me], g_sem)

    def send(chunk, q, to, sem):
        return pltpu.make_async_remote_copy(
            xbuf.at[chunk, q], xbuf.at[chunk, q], sem.at[chunk, q], recv.at[chunk, q],
            device_id={"own": to}, device_id_type=MESH)

    def send_g(chunk, to, sem):
        return pltpu.make_async_remote_copy(
            gbuf.at[chunk], gbuf.at[chunk], sem.at[chunk], g_recv.at[chunk],
            device_id={"own": to}, device_id_type=MESH)

    own_g.start()
    for q in range(pieces):
        own_piece(q).start()
    for q in range(pieces):
        basis_piece(q).start()

    barrier = pltpu.get_barrier_semaphore()

    @pl.when(has_left)
    def _():
        pl.semaphore_signal(barrier, inc=1, device_id={"own": me - 1}, device_id_type=MESH)

    @pl.when(has_right)
    def _():
        pl.semaphore_signal(barrier, inc=1, device_id={"own": me + 1}, device_id_type=MESH)

    pl.semaphore_wait(barrier, has_left.astype(jnp.int32) + has_right.astype(jnp.int32))

    own_g.wait()

    @pl.when(has_right)
    def _():
        send_g(me, me + 1, g_right).start()

    @pl.when(has_left)
    def _():
        send_g(me, me - 1, g_left).start()

    def send_own(q, carry):
        own_piece(q).wait()

        @pl.when(has_right)
        def _():
            send(me, q, me + 1, right_sem).start()

        @pl.when(has_left)
        def _():
            send(me, q, me - 1, left_sem).start()
        return carry

    lax.fori_loop(0, pieces, send_own, 0)

    acc[...] = jnp.zeros_like(acc)
    proj[...] = jnp.zeros_like(proj)
    corr[...] = jnp.zeros_like(corr)

    def multiply(chunk, q, side):
        def one(t, carry):
            columns = pl.ds(pl.multiple_of(t * tile, tile), tile)
            acc[side, pl.ds(0, rows), columns] += jnp.dot(
                xbuf[chunk, q], bbuf[q, :, columns], preferred_element_type=jnp.float32)
            return carry
        lax.fori_loop(0, slots // tile, one, 0)

    def finish(chunk, side):
        proj[pl.ds(0, rows), :] = jnp.dot(gbuf[chunk], bg_ref[...], preferred_element_type=jnp.float32)
        whole = proj[...]
        row = lax.broadcasted_iota(jnp.int32, whole.shape, 0)
        for image in range(images):
            inside = (row >= image * POS) & (row < (image + 1) * POS)
            masked[:, image * gout:(image + 1) * gout] = jnp.where(inside, whole, 0.0).astype(jnp.bfloat16)

        def one(t, carry):
            columns = pl.ds(pl.multiple_of(t * strip, strip), strip)
            coef = lax.dot_general(
                acc[side, :, columns].astype(jnp.bfloat16), masked[...], (((0,), (0,)), ((), ())),
                preferred_element_type=jnp.float32)
            total = corr[columns, :]
            for image in range(images):
                part = coef[:, image * gout:(image + 1) * gout]
                total = total + part * part
            corr[columns, :] = total
            acc[side, :, columns] = jnp.zeros((acc.shape[1], strip), jnp.float32)
            return carry
        lax.fori_loop(0, slots // strip, one, 0)

    def at_distance(d, carry):
        def chunk_of(side):
            return me - d + 2 * d * side

        def present(side):
            chunk = chunk_of(side)
            return (chunk >= 0) & (chunk < n) & ((d > 0) | (side == 0))

        def on_piece(q, carry):
            def on_side(side, carry):
                chunk = chunk_of(side)

                @pl.when(present(side))
                def _():
                    @pl.when(d == 0)
                    def _():
                        basis_piece(q).wait()

                    @pl.when(d > 0)
                    def _():
                        send(chunk, q, me, right_sem).wait_recv()

                        @pl.when((side == 0) & has_right)
                        def _():
                            send(chunk, q, me + 1, right_sem).start()

                        @pl.when((side == 1) & has_left)
                        def _():
                            send(chunk, q, me - 1, left_sem).start()
                    multiply(chunk, q, side)
                return carry
            return lax.fori_loop(0, 2, on_side, carry)
        lax.fori_loop(0, pieces, on_piece, 0)

        def on_end(side, carry):
            chunk = chunk_of(side)

            @pl.when(present(side))
            def _():
                finish(chunk, side)
            return carry

        def on_grads(side, carry):
            chunk = chunk_of(side)

            @pl.when(present(side) & (d > 0))
            def _():
                send_g(chunk, me, g_right).wait_recv()

                @pl.when((side == 0) & has_right)
                def _():
                    send_g(chunk, me + 1, g_right).start()

                @pl.when((side == 1) & has_left)
                def _():
                    send_g(chunk, me - 1, g_left).start()
            return carry
        lax.fori_loop(0, 2, on_grads, 0)
        lax.fori_loop(0, 2, on_end, 0)
        return carry

    lax.fori_loop(0, n, at_distance, 0)

    def drain(chunk, carry):
        @pl.when((chunk <= me) & has_right)
        def _():
            send_g(chunk, me + 1, g_right).wait_send()

        @pl.when((chunk >= me) & has_left)
        def _():
            send_g(chunk, me - 1, g_left).wait_send()

        def one(q, carry):
            @pl.when((chunk <= me) & has_right)
            def _():
                send(chunk, q, me + 1, right_sem).wait_send()

            @pl.when((chunk >= me) & has_left)
            def _():
                send(chunk, q, me - 1, left_sem).wait_send()
            return carry
        lax.fori_loop(0, pieces, one, 0)
        return carry

    lax.fori_loop(0, n, drain, 0)


def partial_corr(n, patches, grads, basis_g, basis_slots):
    rows, kin = patches.shape
    gout = basis_g.shape[1]
    slots = basis_slots.shape[1]
    width = widest(kin, PIECE)
    pieces = kin // width
    padded = -(-rows // 256) * 256
    images = rows // POS
    dma = pltpu.SemaphoreType.DMA
    return pl.pallas_call(
        functools.partial(project, n, images),
        out_shape=jax.ShapeDtypeStruct((slots, gout), jnp.float32),
        in_specs=[
            pl.BlockSpec(memory_space=pl.ANY),
            pl.BlockSpec(memory_space=pl.ANY),
            pl.BlockSpec(memory_space=pltpu.VMEM),
            pl.BlockSpec(memory_space=pl.ANY),
        ],
        out_specs=pl.BlockSpec(memory_space=pltpu.VMEM),
        scratch_shapes=[
            pltpu.VMEM((n, pieces, rows, width), jnp.bfloat16),
            pltpu.VMEM((n, rows, gout), jnp.bfloat16),
            pltpu.VMEM((pieces, width, slots), jnp.bfloat16),
            pltpu.VMEM((2, padded, slots), jnp.float32),
            pltpu.VMEM((padded, gout), jnp.float32),
            pltpu.VMEM((padded, images * gout), jnp.bfloat16),
            dma((pieces,)), dma, dma((pieces,)),
            dma((n, pieces)), dma((n,)), dma((n, pieces)), dma((n, pieces)), dma((n,)), dma((n,)),
        ],
        compiler_params=pltpu.CompilerParams(
            collective_id=0, has_side_effects=True, vmem_limit_bytes=60 * 1024 * 1024),
    )(patches, grads, basis_g, basis_slots)


def shards(patches, grads, basis_g, basis_slots, col_counts):
    groups = lax.axis_size("img")
    owners = lax.axis_size("own")
    owner_id = lax.axis_index("own")
    kin, slots = basis_slots.shape
    gout = basis_g.shape[1]
    total_images = patches.shape[0] // POS * groups * owners
    corr = partial_corr(owners, patches, grads, basis_g, basis_slots)
    starts = jnp.cumsum(col_counts) - col_counts
    my_count = lax.dynamic_index_in_dim(col_counts, owner_id, keepdims=False)
    my_start = lax.dynamic_index_in_dim(starts, owner_id, keepdims=False)
    shift = lax.rem(my_start, jnp.int32(slots))
    rolled = lax.dynamic_slice_in_dim(jnp.concatenate([corr, corr], axis=0), slots - shift, slots, 0)
    kept = lax.psum_scatter(rolled, "img", scatter_dimension=0, tiled=True) / jnp.float32(total_images)
    held = slots // groups
    wraps = kin // slots
    block = kin // (groups * owners)
    subs = held // block
    position = lax.axis_index("img") * held + jnp.arange(held, dtype=jnp.int32)
    final = position[None, :] + jnp.arange(wraps, dtype=jnp.int32)[:, None] * slots
    valid = (final >= my_start) & (final < my_start + my_count)
    laid = jnp.where(valid[:, :, None], kept[None], jnp.float32(0.0)).reshape(owners * block, gout)
    mine = lax.psum_scatter(laid, "own", scatter_dimension=0, tiled=True)
    moves = []
    for j in range(groups):
        for o in range(owners):
            moves.append((j * owners + o, (o // subs) * (slots // block) + j * subs + o % subs))
    return lax.ppermute(mine, ("img", "own"), moves)


def solution(mesh):
    in_specs = (P(("img", "own"), None), P(("img", "own"), None), P(), P(None, "own"), P())
    out_specs = P(("img", "own"), None)
    return jax.shard_map(shards, mesh=mesh, in_specs=in_specs, out_specs=out_specs, check_vma=False)
```

time: 351 us -> 273 us (0.78); the launches traced: 349 us -> 268 us
  Pallas kernels: 0 us -> 150 us
  waiting for transfers between devices: 228 us -> 85.5 us
  matrix products: 37.8 us -> 0 us
  local copies, waits for them, and re-layouts: 37.9 us -> 2.74 us
  blocking collectives: 22.4 us -> 0 us
    pallas_call x0 -> x1, Pallas kernels: none -> 150 us  [partial_corr(): pl.pallas_call(functools.partial(project, n, images), out_shape=jax.Shape...]
    all_gather x1 -> x0, waiting for transfers between devices: 116 us -> none  [shards(): lax.all_gather(patches, 'own', axis=0, tiled=True)]
    psum x1 -> x0, waiting for transfers between devices: 81.4 us -> none  [shards(): summed = lax.psum(slot_corr, 'img')]
    reduce_scatter x1 -> x2, waiting for transfers between devices: 29.4 us -> 80.3 us  [the longest x1 51 us: shards(): lax.psum_scatter(rolled, 'img', scatter_dimension=0, tiled=True)]
    dot_general x3 -> x0, matrix products: 37.8 us -> none  [the longest x1 23.4 us: shards(): jnp.dot(lax.all_gather(patches, 'own', axis=0, tiled=True), basis_slots,...]
    all_gather x1 -> x0, blocking collectives: 22.4 us -> none  [shards(): proj_g = lax.all_gather(proj_local, 'own', axis=0, tiled=True)]
    dynamic_update_slice x1 -> x0, local copies, waits for them, and re-layouts: 13.2 us -> none  [shards(): lax.dynamic_update_slice(jnp.zeros((kin + slots, gout), jnp.float32), mas...]
    broadcast_in_dim x1 -> x0, local copies, waits for them, and re-layouts: 6.88 us -> none  [shards(): jnp.zeros((kin + slots, gout), jnp.float32)]
where the time goes in v1:
time: 273 us; the launch traced here: 268 us
  Pallas kernels  150 us (55%)
  waiting for transfers between devices  85.5 us (31%)
  between operations  15.4 us (6%)
  other arithmetic  10.8 us (4%)
  starting transfers between devices  3.62 us (1%)
  local copies, waits for them, and re-layouts  2.74 us (1%)
    pallas_call x1, Pallas kernels, partial_corr(): pl.pallas_call(functools.partial(project, n, images), out_shape=jax.Shape...  150 us
    reduce_scatter x1, waiting for transfers between devices, shards(): lax.psum_scatter(rolled, 'img', scatter_dimension=0, tiled=True)  51 us
    reduce_scatter x1, waiting for transfers between devices, shards(): mine = lax.psum_scatter(laid, 'own', scatter_dimension=0, tiled=True)  29.3 us
    concatenate x1, other arithmetic, shards(): jnp.concatenate([corr, corr], axis=0)  6.34 us
  transfers between devices with their start and end apart: 3, of which 3 were waited for; matrix products, arithmetic and copies ran while one was open for 1% of the time, Pallas kernels for 0%

profile of v1, /device:TPU:1, one launch (start us, length us, event | category | flops | bytes accessed | tf_op | source)
XLA Modules:
  0.0 267.5 jit_solution(12261509549183756168)
XLA Ops:
  6.5 0.0 reduce-scatter.3.cloned.1.call-start
  6.5 0.8 reduce-window.9
  7.4 0.7 bitcast_subtract_fusion
  8.0 0.6 dynamic_slice.10
  9.3 149.5 %shard_map.55 = f32[2304,512]{1,0:T(8,128)} custom-call(bf16[196,4608]{1,0:T(8,128)(2,1)} %x_hbm.1, bf16[196,512]{1,0:T(8,128)(2,1)} %g_hbm.1, bf16[512,512]{1,0:T(8,128)(2,1)} %bg_ref.1, bf16[4608,2304]{1,0:T(8,128)(2,1)} %b_hbm.1), custom_call_target="tpu_custom_call" | custom-call | tf_op jit(solution)/shard_map/pallas_call | solution.py:221
  158.8 6.3 %fusion = f32[2304,512]{1,0:T(8,128)} fusion(s32[]{:T(128)S(6)} %select_n.14, f32[2304,512]{1,0:T(8,128)} %shard_map.55), kind=kLoop, calls=%fused_computation.2 | loop fusion | flops 1179648 | bytes 9437188 | tf_op jit(solution)/shard_map/concatenate | solution.py:258
  165.1 0.0 copy-start
  165.1 0.0 reduce-scatter.3.cloned.1.call-update
  165.2 0.0 reduce-scatter.5.cloned.1.call-start
  165.2 0.6 copy-done
  165.8 0.6 dynamic_slice.11
  167.7 0.1 add.50
  167.8 0.1 add.51
  167.8 0.1 add.52
  167.9 0.7 compare_and_fusion
  168.6 51.0 %reduce-scatter.3.cloned.1.call-done = f32[288,512]{1,0:T(8,128)} async-done(((f32[2304,512]{1,0:T(8,128)}), f32[288,512]{1,0:T(8,128)}) %reduce-scatter.3.cloned.1.call-update) | async-done | bytes 589840 | tf_op jit(solution)/shard_map/reduce_scatter | solution.py:259
  219.6 1.1 broadcast_multiply_fusion
  220.7 1.2 bitcast_select_fusion
  221.9 0.0 reduce-scatter.5.cloned.1.call-update
  221.9 29.3 %reduce-scatter.5.cloned.1.call-done = f32[144,512]{1,0:T(8,128)} async-done(((f32[576,512]{1,0:T(8,128)}), f32[144,512]{1,0:T(8,128)}) %reduce-scatter.5.cloned.1.call-update) | async-done | bytes 294928 | tf_op jit(solution)/shard_map/reduce_scatter | solution.py:268
  251.2 3.6 %collective-permute-start = (f32[144,512]{1,0:T(8,128)}, f32[144,512]{1,0:T(8,128)S(1)}, u32[]{:S(2)}, u32[]{:S(2)}) collective-permute-start(f32[144,512]{1,0:T(8,128)} %reduce-scatter.5.cloned.1.call-done), channel_id=1, source_target_pairs={{0,0},{1,1},{2,16},{3,17},{4,2},{5,3},{6,18},{7,19},{8,4},{9,5},{1... | collective-permute-start | bytes 884744 | tf_op jit(solution)/shard_map/ppermute | solution.py:273
  254.8 5.2 %collective-permute-done = f32[144,512]{1,0:T(8,128)S(1)} collective-permute-done((f32[144,512]{1,0:T(8,128)}, f32[144,512]{1,0:T(8,128)S(1)}, u32[]{:S(2)}, u32[]{:S(2)}) %collective-permute-start) | collective-permute-done | bytes 294944 | tf_op jit(solution)/shard_map/ppermute | solution.py:273
  260.0 0.7 copy.7
  (3 shorter events, 0.0 us)
Async XLA Ops:
  6.5 213.1 %reduce-scatter.3.cloned.1.call-start = ((), (), s32[]{:S(2)}) async-start(), calls=%async_computation.2 | async-start | bytes 5308416 | tf_op jit(solution)/shard_map/reduce_scatter | solution.py:259
  165.1 0.7 copy-start
  165.2 86.0 %reduce-scatter.5.cloned.1.call-start = ((), (), s32[]{:S(2)}) async-start(), calls=%async_computation.3 | async-start | bytes 1474560 | tf_op jit(solution)/shard_map/reduce_scatter | solution.py:268
  251.2 8.8 %collective-permute-start = (f32[144,512]{1,0:T(8,128)}, f32[144,512]{1,0:T(8,128)S(1)}, u32[]{:S(2)}, u32[]{:S(2)}) collective-permute-start(f32[144,512]{1,0:T(8,128)} %reduce-scatter.5.cloned.1.call-done), channel_id=1, source_target_pairs={{0,0},{1,1},{2,16},{3,17},{4,2},{5,3},{6,18},{7,19},{8,4},{9,5},{1... | collective-permute-start | bytes 884744 | tf_op jit(solution)/shard_map/ppermute | solution.py:273
Sparse Core Ops, SparseCore 0:
  165.3 54.2 reduce-scatter.2
  222.1 29.0 reduce-scatter.4

commit v2 on v1

--- a/solution.py
+++ b/solution.py
@@ -243,34 +243,201 @@
     )(patches, grads, basis_g, basis_slots)
 
 
+def spread(n, groups, wraps, halves, total_images, counts, x_ref, out_ref, *scratch):
+    bits = groups.bit_length() - 1
+    recv, sums = scratch[:bits], scratch[bits:2 * bits]
+    send_sem, recv_sem = scratch[2 * bits:3 * bits], scratch[3 * bits:4 * bits]
+    collected, final, landed, z_send, z_recv, y_send, y_recv = scratch[4 * bits:]
+    j, o = lax.axis_index("img"), lax.axis_index("own")
+    blocks, rows, gout = x_ref.shape
+    part = gout // halves
+    run = groups // wraps
+    streams = blocks // groups
+    level = j // run
+    bit = [(j // 2 ** b) % 2 for b in range(bits)]
+    orders = [[0] + list(range(1, bits)), [0] + list(range(bits - 1, 0, -1))]
+
+    def partner(b):
+        return j + 2 ** b - 2 ** (b + 1) * bit[b]
+
+    def cols(h):
+        return pl.ds(h * part, part)
+
+    barrier = pltpu.get_barrier_semaphore()
+    greeted = 0
+    for b in range(bits):
+        pl.semaphore_signal(barrier, inc=1, device_id={"img": partner(b)}, device_id_type=MESH)
+        greeted += 1
+    for step in range(1, n):
+        pl.semaphore_signal(barrier, inc=1, device_id={"own": lax.rem(o + step, n)}, device_id_type=MESH)
+        greeted += 1
+    for step in range(1, wraps):
+        pl.semaphore_signal(barrier, inc=1, device_id={"img": lax.rem(j + step * run, groups)}, device_id_type=MESH)
+        greeted += 1
+    pl.semaphore_wait(barrier, greeted)
+
+    def block_of(owner, stream):
+        return n * (owner % run) + (owner // run + owner) % wraps + wraps * stream
+
+    def source(stream, t, e, flip):
+        order = orders[stream]
+        if t == 0:
+            owner = 0
+            for i, b in enumerate(order):
+                if i == 0:
+                    value = 1 - bit[b] if flip else bit[b]
+                else:
+                    value = (e >> (i - 1)) & 1
+                owner = owner + value * 2 ** b
+            return x_ref.at[block_of(owner, stream)]
+        value = 1 - bit[order[t]] if flip else bit[order[t]]
+        return sums[t - 1].at[stream, value + 2 * e]
+
+    def exchange(stream, t, e, h):
+        return pltpu.make_async_remote_copy(
+            source(stream, t, e, True).at[:, cols(h)], recv[t].at[stream, e, :, cols(h)],
+            send_sem[t].at[stream, e, h], recv_sem[t].at[stream, e, h],
+            device_id={"img": partner(orders[stream][t])}, device_id_type=MESH)
+
+    def fan(t):
+        return groups >> (t + 1)
+
+    for h in range(halves):
+        for stream in range(streams):
+            for e in range(fan(0)):
+                exchange(stream, 0, e, h).start()
+
+    collects = [o == (level + j) % wraps + wraps * stream for stream in range(streams)]
+    collector = collects[0]
+    for other in collects[1:]:
+        collector = collector | other
+
+    def to_collector(stream, h):
+        return pltpu.make_async_remote_copy(
+            sums[bits - 1].at[stream, 0, :, cols(h)], collected.at[o, :, cols(h)],
+            z_send.at[stream, h], z_recv.at[o, h],
+            device_id={"own": (level + j) % wraps + wraps * stream}, device_id_type=MESH)
+
+    for t in range(bits):
+        for h in range(halves):
+            for stream in range(streams):
+                for e in range(fan(t)):
+                    exchange(stream, t, e, h).wait_recv()
+                    sums[t][stream, e, :, cols(h)] = (
+                        source(stream, t, e, False)[:, cols(h)] + recv[t][stream, e, :, cols(h)])
+                if t + 1 < bits:
+                    for e in range(fan(t + 1)):
+                        exchange(stream, t + 1, e, h).start()
+                else:
+                    @pl.when(collects[stream])
+                    def _():
+                        collected[o, :, cols(h)] = sums[t][stream, 0, :, cols(h)]
+
+                    @pl.when(jnp.logical_not(collects[stream]))
+                    def _():
+                        to_collector(stream, h).start()
+
+    def onward(wrap, h):
+        return pltpu.make_async_remote_copy(
+            final.at[wrap, :, cols(h)], landed.at[:, cols(h)], y_send.at[wrap, h], y_recv.at[h],
+            device_id={"img": j % run + run * wrap}, device_id_type=MESH)
+
+    first, begins = jnp.int32(0), []
+    for owner in range(n):
+        begins.append(first)
+        first = first + counts[owner]
+
+    for h in range(halves):
+        @pl.when(collector)
+        def _():
+            for step in range(1, n):
+                who = lax.rem(o + step, n)
+                pltpu.make_async_remote_copy(
+                    collected.at[who, :, cols(h)], collected.at[who, :, cols(h)],
+                    z_send.at[0, h], z_recv.at[who, h],
+                    device_id={"own": who}, device_id_type=MESH).wait_recv()
+            for wrap in range(wraps):
+                row = (wrap * blocks + n * (j % run) + o) * rows + lax.broadcasted_iota(
+                    jnp.int32, (rows, part), 0)
+                value = jnp.zeros((rows, part), jnp.float32)
+                for owner in range(n):
+                    mine = (row >= begins[owner]) & (row < begins[owner] + counts[owner])
+                    value = jnp.where(mine, collected[owner, :, cols(h)], value)
+                final[wrap, :, cols(h)] = value / jnp.float32(total_images)
+
+                @pl.when(level != wrap)
+                def _():
+                    onward(wrap, h).start()
+
+                @pl.when(level == wrap)
+                def _():
+                    out_ref[:, cols(h)] = final[wrap, :, cols(h)]
+
+    from_self = lax.rem(o - j + wraps * (groups + 1), wraps) == level
+    for h in range(halves):
+        @pl.when(jnp.logical_not(from_self))
+        def _():
+            onward(0, h).wait_recv()
+            out_ref[:, cols(h)] = landed[:, cols(h)]
+
+    for h in range(halves):
+        for stream in range(streams):
+            for t in range(bits):
+                for e in range(fan(t)):
+                    exchange(stream, t, e, h).wait_send()
+
+            @pl.when(jnp.logical_not(collects[stream]))
+            def _():
+                to_collector(stream, h).wait_send()
+        for wrap in range(wraps):
+            @pl.when(collector & (level != wrap))
+            def _():
+                onward(wrap, h).wait_send()
+
+
+def reduce_and_place(n, groups, kin, total_images, rolled, col_counts):
+    slots, gout = rolled.shape
+    wraps = kin // slots
+    rows = kin // (groups * n)
+    blocks = slots // rows
+    streams = blocks // groups
+    bits = groups.bit_length() - 1
+    halves = 2
+    dma = pltpu.SemaphoreType.DMA
+    fans = [groups >> (t + 1) for t in range(bits)]
+    buffers = [pltpu.VMEM((streams, fan, rows, gout), jnp.float32) for fan in fans]
+    sems = [dma((streams, fan, halves)) for fan in fans]
+    return pl.pallas_call(
+        functools.partial(spread, n, groups, wraps, halves, total_images),
+        out_shape=jax.ShapeDtypeStruct((rows, gout), jnp.float32),
+        in_specs=[
+            pl.BlockSpec(memory_space=pltpu.SMEM),
+            pl.BlockSpec(memory_space=pltpu.VMEM),
+        ],
+        out_specs=pl.BlockSpec(memory_space=pltpu.VMEM),
+        scratch_shapes=[
+            *buffers, *buffers, *sems, *sems,
+            pltpu.VMEM((n, rows, gout), jnp.float32),
+            pltpu.VMEM((wraps, rows, gout), jnp.float32),
+            pltpu.VMEM((rows, gout), jnp.float32),
+            dma((streams, halves)), dma((n, halves)), dma((wraps, halves)), dma((halves,)),
+        ],
+        compiler_params=pltpu.CompilerParams(
+            collective_id=1, has_side_effects=True, vmem_limit_bytes=40 * 1024 * 1024),
+    )(col_counts, rolled.reshape(blocks, rows, gout))
+
+
 def shards(patches, grads, basis_g, basis_slots, col_counts):
     groups = lax.axis_size("img")
     owners = lax.axis_size("own")
-    owner_id = lax.axis_index("own")
     kin, slots = basis_slots.shape
-    gout = basis_g.shape[1]
     total_images = patches.shape[0] // POS * groups * owners
     corr = partial_corr(owners, patches, grads, basis_g, basis_slots)
     starts = jnp.cumsum(col_counts) - col_counts
-    my_count = lax.dynamic_index_in_dim(col_counts, owner_id, keepdims=False)
-    my_start = lax.dynamic_index_in_dim(starts, owner_id, keepdims=False)
+    my_start = lax.dynamic_index_in_dim(starts, lax.axis_index("own"), keepdims=False)
     shift = lax.rem(my_start, jnp.int32(slots))
     rolled = lax.dynamic_slice_in_dim(jnp.concatenate([corr, corr], axis=0), slots - shift, slots, 0)
-    kept = lax.psum_scatter(rolled, "img", scatter_dimension=0, tiled=True) / jnp.float32(total_images)
-    held = slots // groups
-    wraps = kin // slots
-    block = kin // (groups * owners)
-    subs = held // block
-    position = lax.axis_index("img") * held + jnp.arange(held, dtype=jnp.int32)
-    final = position[None, :] + jnp.arange(wraps, dtype=jnp.int32)[:, None] * slots
-    valid = (final >= my_start) & (final < my_start + my_count)
-    laid = jnp.where(valid[:, :, None], kept[None], jnp.float32(0.0)).reshape(owners * block, gout)
-    mine = lax.psum_scatter(laid, "own", scatter_dimension=0, tiled=True)
-    moves = []
-    for j in range(groups):
-        for o in range(owners):
-            moves.append((j * owners + o, (o // subs) * (slots // block) + j * subs + o % subs))
-    return lax.ppermute(mine, ("img", "own"), moves)
+    return reduce_and_place(owners, groups, kin, total_images, rolled, col_counts)
 
 
 def solution(mesh):

time: 273 us -> 199 us (0.73); the launches traced: 268 us -> 199 us
  waiting for transfers between devices: 85.5 us -> 0 us
  Pallas kernels: 150 us -> 191 us
  between operations: 15.4 us -> 0.7 us
  other arithmetic: 10.8 us -> 5.69 us
  starting transfers between devices: 3.62 us -> 0 us
    reduce_scatter x2 -> x0, waiting for transfers between devices: 80.3 us -> none  [the longest x1 51 us: shards(): lax.psum_scatter(rolled, 'img', scatter_dimension=0, tiled=True)]
    pallas_call x0 -> x1, Pallas kernels: none -> 41.4 us  [reduce_and_place(): pl.pallas_call(functools.partial(spread, n, groups, wraps, halves, total_...]
    ppermute x1 -> x0, waiting for transfers between devices: 5.17 us -> none  [shards(): return lax.ppermute(mine, ('img', 'own'), moves)]
    ppermute x1 -> x0, starting transfers between devices: 3.58 us -> none  [shards(): return lax.ppermute(mine, ('img', 'own'), moves)]
  transfers between devices with their start and end apart: 3 -> 0, of which waited for: 3 -> 0; matrix products, arithmetic and copies ran while one was open for 1% -> 0% of each run, Pallas kernels for 0% -> 0%
where the time goes in v2:
time: 199 us
  Pallas kernels  191 us (96%)
  other arithmetic  5.69 us (3%)
    pallas_call x1, Pallas kernels, partial_corr(): pl.pallas_call(functools.partial(project, n, images), out_shape=jax.Shape...  149 us
    pallas_call x1, Pallas kernels, reduce_and_place(): pl.pallas_call(functools.partial(spread, n, groups, wraps, halves, total_...  41.4 us
    concatenate x1, other arithmetic, shards(): jnp.concatenate([corr, corr], axis=0)  4.21 us

profile of v2, /device:TPU:1, one launch (start us, length us, event | category | flops | bytes accessed | tf_op | source)
XLA Modules:
  0.0 198.5 jit_solution(7518644095741884776)
XLA Ops:
  0.0 0.8 reduce-window.9
  0.8 0.7 bitcast_subtract_fusion
  1.5 0.6 dynamic_slice.7
  2.7 149.5 %shard_map.55 = f32[2304,512]{1,0:T(8,128)} custom-call(bf16[196,4608]{1,0:T(8,128)(2,1)} %x_hbm.1, bf16[196,512]{1,0:T(8,128)(2,1)} %g_hbm.1, bf16[512,512]{1,0:T(8,128)(2,1)} %bg_ref.1, bf16[4608,2304]{1,0:T(8,128)(2,1)} %b_hbm.1), custom_call_target="tpu_custom_call" | custom-call | tf_op jit(solution)/shard_map/pallas_call | solution.py:221
  152.2 0.0 copy-start
  152.2 4.2 %fusion = f32[2304,512]{1,0:T(8,128)S(1)} fusion(s32[]{:T(128)S(6)} %select_n.8, f32[2304,512]{1,0:T(8,128)} %shard_map.55), kind=kLoop, calls=%fused_computation.2 | loop fusion | flops 1179648 | bytes 9437188 | tf_op jit(solution)/shard_map/concatenate | solution.py:439
  156.4 0.0 copy-done
  156.5 41.4 %shard_map.56 = f32[144,512]{1,0:T(8,128)S(1)} custom-call(s32[4]{0:T(128)S(1)} %copy-done, f32[16,144,512]{2,1,0:T(8,128)S(1)} %bitcast.6), custom_call_target="tpu_custom_call" | custom-call | tf_op jit(solution)/shard_map/pallas_call | solution.py:410
  197.8 0.7 copy.7
Async XLA Ops:
  152.2 4.2 %copy-start = (s32[4]{0:T(128)S(1)}, s32[4]{0:T(128)}, u32[]{:S(2)}) copy-start(s32[4]{0:T(128)} %counts.1) | copy-start | bytes 52

commit v3 on v2

--- a/solution.py
+++ b/solution.py
@@ -16,7 +16,7 @@
     return max(w for w in range(128, most + 1, 128) if total % w == 0)
 
 
-def project(n, images, x_hbm, g_hbm, bg_ref, b_hbm, corr, xbuf, gbuf, bbuf, acc, proj, masked,
+def project(n, images, greet, x_hbm, g_hbm, bg_ref, b_hbm, corr, xbuf, gbuf, bbuf, acc, proj, masked,
             x_sem, g_sem, b_sem, recv, g_recv, right_sem, left_sem, g_right, g_left):
     me = lax.axis_index("own")
     pieces, width, slots = bbuf.shape
@@ -52,18 +52,7 @@
     for q in range(pieces):
         basis_piece(q).start()
 
-    barrier = pltpu.get_barrier_semaphore()
-
-    @pl.when(has_left)
-    def _():
-        pl.semaphore_signal(barrier, inc=1, device_id={"own": me - 1}, device_id_type=MESH)
-
-    @pl.when(has_right)
-    def _():
-        pl.semaphore_signal(barrier, inc=1, device_id={"own": me + 1}, device_id_type=MESH)
-
-    pl.semaphore_wait(barrier, has_left.astype(jnp.int32) + has_right.astype(jnp.int32))
-
+    greet()
     own_g.wait()
 
     @pl.when(has_right)
@@ -113,11 +102,12 @@
             coef = lax.dot_general(
                 acc[side, :, columns].astype(jnp.bfloat16), masked[...], (((0,), (0,)), ((), ())),
                 preferred_element_type=jnp.float32)
-            total = corr[columns, :]
-            for image in range(images):
-                part = coef[:, image * gout:(image + 1) * gout]
-                total = total + part * part
-            corr[columns, :] = total
+            for lane in range(gout // 128):
+                total = corr[lane, columns, :]
+                for image in range(images):
+                    part = coef[:, image * gout + lane * 128:image * gout + (lane + 1) * 128]
+                    total = total + part * part
+                corr[lane, columns, :] = total
             acc[side, :, columns] = jnp.zeros((acc.shape[1], strip), jnp.float32)
             return carry
         lax.fori_loop(0, slots // strip, one, 0)
@@ -206,44 +196,11 @@
         lax.fori_loop(0, pieces, one, 0)
         return carry
 
-    lax.fori_loop(0, n, drain, 0)
-
-
-def partial_corr(n, patches, grads, basis_g, basis_slots):
-    rows, kin = patches.shape
-    gout = basis_g.shape[1]
-    slots = basis_slots.shape[1]
-    width = widest(kin, PIECE)
-    pieces = kin // width
-    padded = -(-rows // 256) * 256
-    images = rows // POS
-    dma = pltpu.SemaphoreType.DMA
-    return pl.pallas_call(
-        functools.partial(project, n, images),
-        out_shape=jax.ShapeDtypeStruct((slots, gout), jnp.float32),
-        in_specs=[
-            pl.BlockSpec(memory_space=pl.ANY),
-            pl.BlockSpec(memory_space=pl.ANY),
-            pl.BlockSpec(memory_space=pltpu.VMEM),
-            pl.BlockSpec(memory_space=pl.ANY),
-        ],
-        out_specs=pl.BlockSpec(memory_space=pltpu.VMEM),
-        scratch_shapes=[
-            pltpu.VMEM((n, pieces, rows, width), jnp.bfloat16),
-            pltpu.VMEM((n, rows, gout), jnp.bfloat16),
-            pltpu.VMEM((pieces, width, slots), jnp.bfloat16),
-            pltpu.VMEM((2, padded, slots), jnp.float32),
-            pltpu.VMEM((padded, gout), jnp.float32),
-            pltpu.VMEM((padded, images * gout), jnp.bfloat16),
-            dma((pieces,)), dma, dma((pieces,)),
-            dma((n, pieces)), dma((n,)), dma((n, pieces)), dma((n, pieces)), dma((n,)), dma((n,)),
-        ],
-        compiler_params=pltpu.CompilerParams(
-            collective_id=0, has_side_effects=True, vmem_limit_bytes=60 * 1024 * 1024),
-    )(patches, grads, basis_g, basis_slots)
-
-
-def spread(n, groups, wraps, halves, total_images, counts, x_ref, out_ref, *scratch):
+    return lambda: lax.fori_loop(0, n, drain, 0)
+
+
+def whole(n, groups, wraps, halves, images, counts, x_hbm, g_hbm, bg_ref, b_hbm, out_ref, corr, x_ref, *scratch):
+    ours, scratch = scratch[:15], scratch[15:]
     bits = groups.bit_length() - 1
     recv, sums = scratch[:bits], scratch[bits:2 * bits]
     send_sem, recv_sem = scratch[2 * bits:3 * bits], scratch[3 * bits:4 * bits]
@@ -263,33 +220,52 @@
     def cols(h):
         return pl.ds(h * part, part)
 
-    barrier = pltpu.get_barrier_semaphore()
-    greeted = 0
-    for b in range(bits):
-        pl.semaphore_signal(barrier, inc=1, device_id={"img": partner(b)}, device_id_type=MESH)
-        greeted += 1
-    for step in range(1, n):
-        pl.semaphore_signal(barrier, inc=1, device_id={"own": lax.rem(o + step, n)}, device_id_type=MESH)
-        greeted += 1
-    for step in range(1, wraps):
-        pl.semaphore_signal(barrier, inc=1, device_id={"img": lax.rem(j + step * run, groups)}, device_id_type=MESH)
-        greeted += 1
-    pl.semaphore_wait(barrier, greeted)
+    def greet():
+        barrier = pltpu.get_barrier_semaphore()
+        greeted = 0
+        for b in range(bits):
+            pl.semaphore_signal(barrier, inc=1, device_id={"img": partner(b)}, device_id_type=MESH)
+            greeted += 1
+        for step in range(1, n):
+            pl.semaphore_signal(barrier, inc=1, device_id={"own": lax.rem(o + step, n)}, device_id_type=MESH)
+            greeted += 1
+        for step in range(1, wraps):
+            pl.semaphore_signal(barrier, inc=1, device_id={"img": lax.rem(j + step * run, groups)}, device_id_type=MESH)
+            greeted += 1
+        pl.semaphore_wait(barrier, greeted)
+
+    drain_rows = project(n, images, greet, x_hbm, g_hbm, bg_ref, b_hbm, corr, *ours)
+
+    slots = blocks * rows
+    corr[:, pl.ds(slots, rows), :] = corr[:, pl.ds(0, rows), :]
+    first, begins, my_start = jnp.int32(0), [], jnp.int32(0)
+    for owner in range(n):
+        begins.append(first)
+        my_start = jnp.where(o == owner, first, my_start)
+        first = first + counts[owner]
+
+    def rotate(block):
+        base = lax.rem(block * rows + (wraps + 1) * slots - my_start, slots)
+        for lane in range(gout // 128):
+            x_ref[block, :, lane * 128:(lane + 1) * 128] = corr[lane, pl.ds(base, rows), :]
 
     def block_of(owner, stream):
         return n * (owner % run) + (owner // run + owner) % wraps + wraps * stream
+
+    def first_block(stream, e, flip):
+        owner = 0
+        for i, b in enumerate(orders[stream]):
+            if i == 0:
+                value = 1 - bit[b] if flip else bit[b]
+            else:
+                value = (e >> (i - 1)) & 1
+            owner = owner + value * 2 ** b
+        return block_of(owner, stream)
 
     def source(stream, t, e, flip):
         order = orders[stream]
         if t == 0:
-            owner = 0
-            for i, b in enumerate(order):
-                if i == 0:
-                    value = 1 - bit[b] if flip else bit[b]
-                else:
-                    value = (e >> (i - 1)) & 1
-                owner = owner + value * 2 ** b
-            return x_ref.at[block_of(owner, stream)]
+            return x_ref.at[first_block(stream, e, flip)]
         value = 1 - bit[order[t]] if flip else bit[order[t]]
         return sums[t - 1].at[stream, value + 2 * e]
 
@@ -302,10 +278,16 @@
     def fan(t):
         return groups >> (t + 1)
 
+    for stream in range(streams):
+        for e in range(fan(0)):
+            rotate(first_block(stream, e, True))
     for h in range(halves):
         for stream in range(streams):
             for e in range(fan(0)):
                 exchange(stream, 0, e, h).start()
+    for stream in range(streams):
+        for e in range(fan(0)):
+            rotate(first_block(stream, e, False))
 
     collects = [o == (level + j) % wraps + wraps * stream for stream in range(streams)]
     collector = collects[0]
@@ -342,11 +324,6 @@
             final.at[wrap, :, cols(h)], landed.at[:, cols(h)], y_send.at[wrap, h], y_recv.at[h],
             device_id={"img": j % run + run * wrap}, device_id_type=MESH)
 
-    first, begins = jnp.int32(0), []
-    for owner in range(n):
-        begins.append(first)
-        first = first + counts[owner]
-
     for h in range(halves):
         @pl.when(collector)
         def _():
@@ -363,7 +340,7 @@
                 for owner in range(n):
                     mine = (row >= begins[owner]) & (row < begins[owner] + counts[owner])
                     value = jnp.where(mine, collected[owner, :, cols(h)], value)
-                final[wrap, :, cols(h)] = value / jnp.float32(total_images)
+                final[wrap, :, cols(h)] = value / jnp.float32(images * groups * n)
 
                 @pl.when(level != wrap)
                 def _():
@@ -393,10 +370,19 @@
             @pl.when(collector & (level != wrap))
             def _():
                 onward(wrap, h).wait_send()
-
-
-def reduce_and_place(n, groups, kin, total_images, rolled, col_counts):
-    slots, gout = rolled.shape
+    drain_rows()
+
+
+def shards(patches, grads, basis_g, basis_slots, col_counts):
+    groups = lax.axis_size("img")
+    n = lax.axis_size("own")
+    kin, slots = basis_slots.shape
+    gout = basis_g.shape[1]
+    patch_rows = patches.shape[0]
+    images = patch_rows // POS
+    padded = -(-patch_rows // 256) * 256
+    width = widest(kin, PIECE)
+    pieces = kin // width
     wraps = kin // slots
     rows = kin // (groups * n)
     blocks = slots // rows
@@ -408,14 +394,27 @@
     buffers = [pltpu.VMEM((streams, fan, rows, gout), jnp.float32) for fan in fans]
     sems = [dma((streams, fan, halves)) for fan in fans]
     return pl.pallas_call(
-        functools.partial(spread, n, groups, wraps, halves, total_images),
+        functools.partial(whole, n, groups, wraps, halves, images),
         out_shape=jax.ShapeDtypeStruct((rows, gout), jnp.float32),
         in_specs=[
             pl.BlockSpec(memory_space=pltpu.SMEM),
+            pl.BlockSpec(memory_space=pl.ANY),
+            pl.BlockSpec(memory_space=pl.ANY),
             pl.BlockSpec(memory_space=pltpu.VMEM),
+            pl.BlockSpec(memory_space=pl.ANY),
         ],
         out_specs=pl.BlockSpec(memory_space=pltpu.VMEM),
         scratch_shapes=[
+            pltpu.VMEM((gout // 128, slots + rows, 128), jnp.float32),
+            pltpu.VMEM((blocks, rows, gout), jnp.float32),
+            pltpu.VMEM((n, pieces, patch_rows, width), jnp.bfloat16),
+            pltpu.VMEM((n, patch_rows, gout), jnp.bfloat16),
+            pltpu.VMEM((pieces, width, slots), jnp.bfloat16),
+            pltpu.VMEM((2, padded, slots), jnp.float32),
+            pltpu.VMEM((padded, gout), jnp.float32),
+            pltpu.VMEM((padded, images * gout), jnp.bfloat16),
+            dma((pieces,)), dma, dma((pieces,)),
+            dma((n, pieces)), dma((n,)), dma((n, pieces)), dma((n, pieces)), dma((n,)), dma((n,)),
             *buffers, *buffers, *sems, *sems,
             pltpu.VMEM((n, rows, gout), jnp.float32),
             pltpu.VMEM((wraps, rows, gout), jnp.float32),
@@ -423,21 +422,8 @@
             dma((streams, halves)), dma((n, halves)), dma((wraps, halves)), dma((halves,)),
         ],
         compiler_params=pltpu.CompilerParams(
-            collective_id=1, has_side_effects=True, vmem_limit_bytes=40 * 1024 * 1024),
-    )(col_counts, rolled.reshape(blocks, rows, gout))
-
-
-def shards(patches, grads, basis_g, basis_slots, col_counts):
-    groups = lax.axis_size("img")
-    owners = lax.axis_size("own")
-    kin, slots = basis_slots.shape
-    total_images = patches.shape[0] // POS * groups * owners
-    corr = partial_corr(owners, patches, grads, basis_g, basis_slots)
-    starts = jnp.cumsum(col_counts) - col_counts
-    my_start = lax.dynamic_index_in_dim(starts, lax.axis_index("own"), keepdims=False)
-    shift = lax.rem(my_start, jnp.int32(slots))
-    rolled = lax.dynamic_slice_in_dim(jnp.concatenate([corr, corr], axis=0), slots - shift, slots, 0)
-    return reduce_and_place(owners, groups, kin, total_images, rolled, col_counts)
+            collective_id=0, has_side_effects=True, vmem_limit_bytes=67043328),
+    )(col_counts, patches, grads, basis_g, basis_slots)
 
 
 def solution(mesh):

time: 199 us -> 190 us (0.955)
  other arithmetic: 5.69 us -> 0 us
  Pallas kernels: 191 us -> 187 us
    concatenate x1 -> x0, other arithmetic: 4.21 us -> none  [shards(): jnp.concatenate([corr, corr], axis=0)]
    pallas_call x2 -> x1, Pallas kernels: 191 us -> 187 us  [shards(): pl.pallas_call(functools.partial(whole, n, groups, wraps, halves, images)...]
where the time goes in v3:
time: 190 us; the launch traced here: 189 us
  Pallas kernels  187 us (98%)
    pallas_call x1, Pallas kernels, shards(): pl.pallas_call(functools.partial(whole, n, groups, wraps, halves, images)...  187 us

profile of v3, /device:TPU:1, one launch (start us, length us, event | category | flops | bytes accessed | tf_op | source)
XLA Modules:
  0.0 188.9 jit_solution(9484304785166730632)
XLA Ops:
  0.0 187.2 %shard_map.55 = f32[144,512]{1,0:T(8,128)} custom-call(s32[4]{0:T(128)} %counts.1, bf16[196,4608]{1,0:T(8,128)(2,1)} %x_hbm.1, bf16[196,512]{1,0:T(8,128)(2,1)} %g_hbm.1, bf16[512,512]{1,0:T(8,128)(2,1)} %bg_ref.1, bf16[4608,2304]{1,0:T(8,128)(2,1)} %b_hbm.1), custom_call_target="tpu_custom_call" | custom-call | tf_op jit(solution)/shard_map/pallas_call | solution.py:396
  187.2 1.7 copy.7

commit v4 on v3

--- a/solution.py
+++ b/solution.py
@@ -388,7 +388,7 @@
     blocks = slots // rows
     streams = blocks // groups
     bits = groups.bit_length() - 1
-    halves = 2
+    halves = 4
     dma = pltpu.SemaphoreType.DMA
     fans = [groups >> (t + 1) for t in range(bits)]
     buffers = [pltpu.VMEM((streams, fan, rows, gout), jnp.float32) for fan in fans]

time: 190 us -> 188 us (0.989)
  no operation moved by 1% of the time
where the time goes in v4:
time: 188 us
  Pallas kernels  186 us (99%)
    pallas_call x1, Pallas kernels, shards(): pl.pallas_call(functools.partial(whole, n, groups, wraps, halves, images)...  186 us

profile of v4, /device:TPU:1, one launch (start us, length us, event | category | flops | bytes accessed | tf_op | source)
XLA Modules:
  0.0 188.1 jit_solution(8887140964893622556)
XLA Ops:
  0.0 186.4 %shard_map.55 = f32[144,512]{1,0:T(8,128)} custom-call(s32[4]{0:T(128)} %counts.1, bf16[196,4608]{1,0:T(8,128)(2,1)} %x_hbm.1, bf16[196,512]{1,0:T(8,128)(2,1)} %g_hbm.1, bf16[512,512]{1,0:T(8,128)(2,1)} %bg_ref.1, bf16[4608,2304]{1,0:T(8,128)(2,1)} %b_hbm.1), custom_call_target="tpu_custom_call" | custom-call | tf_op jit(solution)/shard_map/pallas_call | solution.py:396
  186.4 1.7 copy.7
